TPU v7x, 32 devices: a whole 2x2x4 slice. The times are simulated.
32 devices in a mesh: row: 8 (over z, y), col: 4 (over x, core).
Axes of the slice: x: 2, y: 2, z: 4, core: 2. Of those that a mesh axis runs over, the one named last changes fastest.
Arguments:
- inputs: bfloat16 [768, 8192], P('row', 'col'), may hold values from -16 to 16
- norm_gain: float32 [8192], P('col'), may hold values from 0.25 to 4
- w_gate: bfloat16 [8192, 28672], P('col', 'row'), may hold values from -0.09375 to 0.09375
- w_up: bfloat16 [8192, 28672], P('col', 'row'), may hold values from -0.09375 to 0.09375
- w_down: bfloat16 [28672, 8192], P('row', 'col'), may hold values from -0.050111483 to 0.050111483
- mask_gate: int32 [128, 448], P('col', 'row'), may hold values 0 or 1
- mask_up: int32 [128, 448], P('col', 'row'), may hold values 0 or 1
- mask_down: int32 [448, 128], P('row', 'col'), may hold values 0 or 1
- grad_out: bfloat16 [768, 8192], P('row', 'col'), may hold values from -5 to 5
Outputs:
- output: bfloat16 [768, 8192], P('row', 'col')
- grad_inputs: bfloat16 [768, 8192], P('row', 'col')
- grad_gain: float32 [8192], P('col')
- grad_w_gate: bfloat16 [8192, 28672], P('col', 'row')
- grad_w_up: bfloat16 [8192, 28672], P('col', 'row')
- grad_w_down: bfloat16 [28672, 8192], P('row', 'col')
All inputs are finite; a program needn't handle non-finite values. No bound on the sum of `mask_gate` or of `mask_up` or of `mask_down` on one device may be relied on, other than what follows from the above.
Results may differ from a plain program's by a relative error of at most 0.02.
Values may be sent and summed in bfloat16 or wider, within the bound.
No kernel may reach another device: no remote copies, remote signals or barrier semaphores. Data moves between devices by JAX's collectives and lax.ppermute only.
A program may use at most 256 MiB of HBM per device.

v0:
```python
import jax
import jax.numpy as jnp
from jax import lax
from jax.sharding import PartitionSpec as P

D = 8192
BLOCK = 64
epsilon = 1e-05


def expand_mask(weight, block_mask):
    mask_rows, mask_cols = block_mask.shape
    blocked = (
        weight.reshape(mask_rows, BLOCK, mask_cols, BLOCK)
        * block_mask.astype(jnp.bfloat16)[:, None, :, None]
    )
    return blocked.reshape(weight.shape)


def contract_rows(left, right):
    return lax.dot_general(
        left, right, (((0,), (0,)), ((), ())), preferred_element_type=jnp.float32
    )


def contract_cols(left, right):
    return lax.dot_general(
        left, right, (((1,), (1,)), ((), ())), preferred_element_type=jnp.float32
    )


def shards(inputs, norm_gain, w_gate, w_up, w_down, mask_gate, mask_up, mask_down, grad_out):
    gate_eff = expand_mask(w_gate, mask_gate)
    up_eff = expand_mask(w_up, mask_up)
    down_eff = expand_mask(w_down, mask_down)
    local_rows = inputs.shape[0]
    inputs_all, grads_all = (
        lax.all_gather(inputs, "row", axis=0, tiled=True),
        lax.all_gather(grad_out, "row", axis=0, tiled=True),
    )
    ff_width = w_gate.shape[1]
    inputs_wide = inputs_all.astype(jnp.float32)
    squares = lax.psum(jnp.sum(inputs_wide * inputs_wide, axis=1, keepdims=True), "col")
    inv_rms = lax.rsqrt(squares / D + epsilon)
    normed = inputs_wide * inv_rms
    hidden_in = (normed * norm_gain).astype(jnp.bfloat16)
    row_block = hidden_in
    projected = lax.psum_scatter(
        jnp.concatenate(
            [
                jnp.dot(row_block, gate_eff, preferred_element_type=jnp.float32),
                jnp.dot(row_block, up_eff, preferred_element_type=jnp.float32),
            ],
            axis=1,
        ).astype(jnp.bfloat16),
        "col",
        scatter_dimension=0,
        tiled=True,
    ).astype(jnp.float32)
    gate_value = projected[:, :ff_width]
    up_value = projected[:, ff_width:]
    sigmoid_gate = jax.nn.sigmoid(gate_value)
    silu_gate = gate_value * sigmoid_gate
    hidden = (silu_gate * up_value).astype(jnp.bfloat16)
    hidden_all = lax.all_gather(hidden, "col", axis=0, tiled=True)
    row_block = hidden_all
    mixed_out = lax.psum_scatter(
        jnp.dot(row_block, down_eff, preferred_element_type=jnp.float32).astype(jnp.bfloat16),
        "row",
        scatter_dimension=0,
        tiled=True,
    ).astype(jnp.float32)
    output = (inputs.astype(jnp.float32) + mixed_out).astype(jnp.bfloat16)
    grad_w_down = expand_mask(contract_rows(hidden_all, grads_all).astype(jnp.bfloat16), mask_down)
    row_block = grads_all
    d_hidden = lax.psum_scatter(
        contract_cols(row_block, down_eff).astype(jnp.bfloat16),
        "col",
        scatter_dimension=0,
        tiled=True,
    ).astype(jnp.float32)
    d_up = (d_hidden * silu_gate).astype(jnp.bfloat16)
    d_gate = (
        d_hidden * up_value * sigmoid_gate * (1.0 + gate_value * (1.0 - sigmoid_gate))
    ).astype(jnp.bfloat16)
    d_gate_all, d_up_all = (
        lax.all_gather(d_gate, "col", axis=0, tiled=True),
        lax.all_gather(d_up, "col", axis=0, tiled=True),
    )
    grad_w_gate = expand_mask(contract_rows(hidden_in, d_gate_all).astype(jnp.bfloat16), mask_gate)
    grad_w_up = expand_mask(contract_rows(hidden_in, d_up_all).astype(jnp.bfloat16), mask_up)
    d_norm_in = lax.psum_scatter(
        (contract_cols(d_gate_all, gate_eff) + contract_cols(d_up_all, up_eff)).astype(
            jnp.bfloat16
        ),
        "row",
        scatter_dimension=0,
        tiled=True,
    ).astype(jnp.float32)
    row_start = lax.axis_index("row") * local_rows
    normed_local = lax.dynamic_slice_in_dim(normed, row_start, local_rows, 0)
    inv_rms_local = lax.dynamic_slice_in_dim(inv_rms, row_start, local_rows, 0)
    gain_part = jnp.sum(d_norm_in * normed_local, axis=0)
    d_normed = d_norm_in * norm_gain
    inner_part = jnp.sum(d_normed * normed_local, axis=1, keepdims=True)
    row_inner = lax.psum(inner_part, "col") / D
    grad_gain = lax.psum(gain_part, "row")
    grad_inputs = (
        grad_out.astype(jnp.float32) + inv_rms_local * (d_normed - normed_local * row_inner)
    ).astype(jnp.bfloat16)
    return (output, grad_inputs, grad_gain, grad_w_gate, grad_w_up, grad_w_down)


def solution(mesh):
    in_specs = (
        P("row", "col"),
        P("col"),
        P("col", "row"),
        P("col", "row"),
        P("row", "col"),
        P("col", "row"),
        P("col", "row"),
        P("row", "col"),
        P("row", "col"),
    )
    out_specs = (
        P("row", "col"),
        P("row", "col"),
        P("col"),
        P("col", "row"),
        P("col", "row"),
        P("row", "col"),
    )
    return jax.shard_map(shards, mesh=mesh, in_specs=in_specs, out_specs=out_specs, check_vma=False)
```

profile of v0, /device:TPU:0, one launch (start us, length us, event | category | flops | bytes accessed | tf_op | source)
XLA Modules:
  0.0 632.4 jit_solution(2924886407965607107)
XLA Ops:
  7.2 0.0 all-gather.6.cloned.1.call-start
  7.2 0.7 all-gather.6.cloned.1.call-update
  7.9 0.0 all-gather.10.cloned.1.call-start
  7.9 0.7 all-gather.10.cloned.1.call-update
  8.6 0.0 reduce-scatter.5.cloned.1.call-start
  8.7 0.7 convert_element_type.77
  9.4 10.0 %mul.142 = bf16[32,64,56,64]{3,2,1,0:T(8,128)(2,1)} broadcast(bf16[32,56]{1,0:T(8,128)(2,1)S(1)} %convert_element_type.77), dimensions={0,2} | broadcast | bytes 14683648 | tf_op jit(solution)/shard_map/mul | solution.py:14
  19.4 36.2 %mul.143 = bf16[2048,3584]{1,0:T(8,128)(2,1)} reshape(bf16[32,64,56,64]{3,2,1,0:T(8,128)(2,1)} %mul.142) | data formatting | bytes 29360128 | tf_op jit(solution)/shard_map/mul | solution.py:14
  55.7 10.1 %mul.139 = bf16[32,64,56,64]{3,2,1,0:T(8,128)(2,1)} broadcast(bf16[32,56]{1,0:T(8,128)(2,1)S(1)} %convert_element_type.76), dimensions={0,2} | broadcast | bytes 14683648 | tf_op jit(solution)/shard_map/mul | solution.py:14
  65.8 36.3 %mul.140 = bf16[2048,3584]{1,0:T(8,128)(2,1)} reshape(bf16[32,64,56,64]{3,2,1,0:T(8,128)(2,1)} %mul.139) | data formatting | bytes 29360128 | tf_op jit(solution)/shard_map/mul | solution.py:14
  102.1 18.6 %mul.144 = bf16[2048,3584]{1,0:T(8,128)(2,1)} multiply(bf16[2048,3584]{1,0:T(8,128)(2,1)} %param.12, bf16[2048,3584]{1,0:T(8,128)(2,1)} %mul.143) | non-fusion elementwise | flops 7340032 | bytes 44040192 | tf_op jit(solution)/shard_map/mul | solution.py:14
  120.7 1.1 copy-done
  121.8 14.7 %mul.141 = bf16[2048,3584]{1,0:T(8,128)(2,1)} multiply(bf16[2048,3584]{1,0:T(8,128)(2,1)} %param.11, bf16[2048,3584]{1,0:T(8,128)(2,1)S(1)} %copy-done) | non-fusion elementwise | flops 7340032 | bytes 44040192 | tf_op jit(solution)/shard_map/mul | solution.py:14
  136.6 2.7 fusion.3
  139.3 8.2 %psum.21 = f32[768,1]{0,1:T(1,128)S(1)} all-reduce(f32[768,1]{0,1:T(1,128)S(1)} %broadcast_in_dim.4), channel_id=1, replica_groups=mesh['row'=8,'col'=4] {'col'}, use_global_device_ids=true, to_apply=%region_1.0 | all-reduce | flops 768 | bytes 6144 | tf_op jit(solution)/shard_map/psum | solution.py:43
  147.5 0.6 fusion.23
  148.1 0.0 copy-done.5
  148.1 0.0 copy-start.1
  148.1 17.5 %convolution_convert_fusion.4 = bf16[768,3584]{1,0:T(8,128)(2,1)} fusion(bf16[2048,3584]{1,0:T(8,128)(2,1)} %mul.144, f32[2048]{0:T(1024)S(1)} %copy-done.5, f32[768]{0:T(1024)S(1)} %get-tuple-element.8, bf16[768,2048]{1,0:T(8,128)(2,1)} %all-gather.6.cloned.1.call-done), kind=kOutput, calls=%fused_computation.10 | convolution fusion | flops 11283333120 | bytes 23342080 | tf_op jit(solution)/shard_map/dot_general | solution.py:52
  165.6 0.0 slice-done
  165.6 13.5 %convolution_convert_fusion.5 = bf16[768,3584]{1,0:T(8,128)(2,1)} fusion(bf16[2048,3584]{1,0:T(8,128)(2,1)S(1)} %bitcast.26, f32[2048]{0:T(1024)S(1)} %copy-done.5, f32[768]{0:T(1024)S(1)} %get-tuple-element.8, bf16[768,2048]{1,0:T(8,128)(2,1)S(1)} %copy-done.1), kind=kOutput, calls=%fused_computation.11 | convolution fusion | flops 11283333120 | bytes 23342080 | tf_op jit(solution)/shard_map/dot_general | solution.py:51
  179.1 9.5 %pad_maximum_fusion = bf16[768,7168]{1,0:T(8,128)(2,1)} fusion(bf16[768,3584]{1,0:T(8,128)(2,1)} %convolution_convert_fusion.4, bf16[768,3584]{1,0:T(8,128)(2,1)} %convolution_convert_fusion.5), kind=kLoop, calls=%fused_computation.6 | loop fusion | flops 22020096 | bytes 22020096 | tf_op jit(solution)/shard_map/concatenate | solution.py:49
  188.6 0.0 reduce-scatter.5.cloned.1.call-update
  188.6 0.5 reduce-scatter.9.cloned.1.call-start
  189.1 0.2 copy-done.8
  189.3 0.1 copy.15
  189.4 14.1 %mul.147 = bf16[56,64,32,64]{3,2,1,0:T(8,128)(2,1)} broadcast(bf16[56,32]{1,0:T(8,128)(2,1)S(1)} %copy.15), dimensions={0,2} | broadcast | bytes 14683648 | tf_op jit(solution)/shard_map/mul | solution.py:14
  203.6 40.8 %mul.148 = bf16[3584,2048]{1,0:T(8,128)(2,1)} reshape(bf16[56,64,32,64]{3,2,1,0:T(8,128)(2,1)} %mul.147) | data formatting | bytes 29360128 | tf_op jit(solution)/shard_map/mul | solution.py:14
  244.4 19.8 %fusion.4 = bf16[768,3584]{1,0:T(8,128)(2,1)} fusion(bf16[768,2048]{1,0:T(8,128)(2,1)} %all-gather.10.cloned.1.call-done, bf16[3584,2048]{1,0:T(8,128)(2,1)} %param.13, bf16[3584,2048]{1,0:T(8,128)(2,1)} %mul.148), kind=kOutput, calls=%fused_computation.15 | convolution fusion | flops 11284381696 | bytes 38010880 | tf_op jit(solution)/shard_map/dot_general | solution.py:27
  264.1 0.0 reduce-scatter.9.cloned.1.call-update
  264.2 0.0 all-gather.12.cloned.1.call-start
  264.2 12.5 %reduce-scatter.5.cloned.1.call-done = bf16[192,7168]{1,0:T(8,128)(2,1)} async-done(((bf16[768,7168]{1,0:T(8,128)(2,1)}), bf16[192,7168]{1,0:T(8,128)(2,1)}) %reduce-scatter.5.cloned.1.call-update) | async-done | bytes 2752528 | tf_op jit(solution)/shard_map/reduce_scatter | solution.py:48
  276.7 4.8 convert_element_type.78
  281.5 50.6 %reduce-scatter.9.cloned.1.call-done = bf16[192,3584]{1,0:T(8,128)(2,1)} async-done(((bf16[768,3584]{1,0:T(8,128)(2,1)}), bf16[192,3584]{1,0:T(8,128)(2,1)}) %reduce-scatter.9.cloned.1.call-update) | async-done | bytes 1376272 | tf_op jit(solution)/shard_map/reduce_scatter | solution.py:76
  332.1 5.0 fusion.14
  337.1 0.0 all-gather.12.cloned.1.call-update
  337.1 0.0 all-gather.14.cloned.1.call-start
  337.2 0.5 all-gather.14.cloned.1.call-update
  337.7 0.0 all-gather.8.cloned.1.call-start
  337.8 0.7 all-gather.8.cloned.1.call-update
  338.5 0.0 reduce-scatter.11.cloned.1.call-start
  338.5 40.7 %all-gather.12.cloned.1.call-done = bf16[768,3584]{1,0:T(8,128)(2,1)} async-done(((bf16[192,3584]{1,0:T(8,128)(2,1)}), bf16[768,3584]{1,0:T(8,128)(2,1)}) %all-gather.12.cloned.1.call-update) | async-done | bytes 5505040 | tf_op jit(solution)/shard_map/all_gather | solution.py:87
  379.2 18.3 %fusion.24 = f32[768,2048]{1,0:T(8,128)} fusion(bf16[768,3584]{1,0:T(8,128)(2,1)} %all-gather.12.cloned.1.call-done, bf16[2048,3584]{1,0:T(8,128)(2,1)} %mul.141), kind=kOutput, calls=%fused_computation.43 | convolution fusion | flops 11274289152 | bytes 26476544 | tf_op jit(solution)/shard_map/dot_general | solution.py:27
  397.5 25.1 %all-gather.14.cloned.1.call-done = bf16[768,3584]{1,0:T(8,128)(2,1)} async-done(((bf16[192,3584]{1,0:T(8,128)(2,1)}), bf16[768,3584]{1,0:T(8,128)(2,1)}) %all-gather.14.cloned.1.call-update) | async-done | bytes 5505040 | tf_op jit(solution)/shard_map/all_gather | solution.py:88
  422.6 18.5 %add_convert_fusion = bf16[768,2048]{1,0:T(8,128)(2,1)} fusion(f32[768,2048]{1,0:T(8,128)} %fusion.24, bf16[768,3584]{1,0:T(8,128)(2,1)} %all-gather.14.cloned.1.call-done, bf16[2048,3584]{1,0:T(8,128)(2,1)} %mul.144), kind=kOutput, calls=%fused_computation.13 | convolution fusion | flops 11277434880 | bytes 29622272 | tf_op jit(solution)/shard_map/dot_general | solution.py:27
  441.1 0.0 reduce-scatter.11.cloned.1.call-update
  441.1 0.2 reduce-scatter.7.cloned.1.call-start
  441.4 0.8 dynamic-slice_bitcast_fusion
  442.1 0.0 copy-done.2
  442.1 3.1 convert_multiply_fusion
  445.2 20.8 %all-gather.8.cloned.1.call-done = bf16[768,3584]{1,0:T(8,128)(2,1)} async-done(((bf16[192,3584]{1,0:T(8,128)(2,1)}), bf16[768,3584]{1,0:T(8,128)(2,1)}) %all-gather.8.cloned.1.call-update) | async-done | bytes 5505040 | tf_op jit(solution)/shard_map/all_gather | solution.py:65
  466.0 19.7 %fusion.8 = bf16[768,2048]{1,0:T(8,128)(2,1)} fusion(bf16[768,3584]{1,0:T(8,128)(2,1)} %all-gather.8.cloned.1.call-done, bf16[3584,2048]{1,0:T(8,128)(2,1)} %param.13, bf16[3584,2048]{1,0:T(8,128)(2,1)} %mul.148), kind=kOutput, calls=%fused_computation.21 | convolution fusion | flops 11283202048 | bytes 38010880 | tf_op jit(solution)/shard_map/dot_general | solution.py:68
  485.7 0.0 reduce-scatter.7.cloned.1.call-update
  485.8 18.6 %fusion = bf16[2048,3584]{1,0:T(8,128)(2,1)} fusion(bf16[2048,3584]{1,0:T(8,128)(2,1)} %mul.140, bf16[768,3584]{1,0:T(8,128)(2,1)} %all-gather.12.cloned.1.call-done, f32[2048]{0:T(1024)S(1)} %copy-done.6, f32[768]{0:T(1024)S(1)} %get-tuple-element.8, bf16[768,2048]{1,0:T(8,128)(2,1)S(1)} %copy-done.2), kind=kOutput, calls=%fused_computation.3 | convolution fusion | flops 11295260672 | bytes 38022144 | tf_op jit(solution)/shard_map/dot_general | solution.py:21
  504.4 18.7 %fusion.1 = bf16[2048,3584]{1,0:T(8,128)(2,1)} fusion(bf16[2048,3584]{1,0:T(8,128)(2,1)} %mul.143, bf16[768,3584]{1,0:T(8,128)(2,1)} %all-gather.14.cloned.1.call-done, f32[2048]{0:T(1024)S(1)} %copy-done.6, f32[768]{0:T(1024)S(1)} %get-tuple-element.8, bf16[768,2048]{1,0:T(8,128)(2,1)S(1)} %copy-done.2), kind=kOutput, calls=%fused_computation.4 | convolution fusion | flops 11295260672 | bytes 38022144 | tf_op jit(solution)/shard_map/dot_general | solution.py:21
  523.1 20.3 %fusion.2 = bf16[3584,2048]{1,0:T(8,128)(2,1)} fusion(bf16[3584,2048]{1,0:T(8,128)(2,1)} %mul.148, bf16[768,3584]{1,0:T(8,128)(2,1)} %all-gather.8.cloned.1.call-done, bf16[768,2048]{1,0:T(8,128)(2,1)} %all-gather.10.cloned.1.call-done), kind=kOutput, calls=%fused_computation.5 | convolution fusion | flops 11288969216 | bytes 38010880 | tf_op jit(solution)/shard_map/dot_general | solution.py:21
  543.4 0.6 reduce-scatter.11.cloned.1.call-done
  544.0 1.5 fusion.22
  545.6 5.9 psum.22
  551.5 22.2 %psum.23 = f32[2048]{0:T(1024)} all-reduce(f32[2048]{0:T(1024)S(1)} %get-tuple-element.6), channel_id=1, replica_groups=mesh['row'=8,'col'=4] {'row'}, use_global_device_ids=true, to_apply=%region_9.0 | all-reduce | flops 2048 | bytes 16384 | tf_op jit(solution)/shard_map/psum | solution.py:107
  573.6 47.9 %reduce-scatter.7.cloned.1.call-done = bf16[96,2048]{1,0:T(8,128)(2,1)} async-done(((bf16[768,2048]{1,0:T(8,128)(2,1)}), bf16[96,2048]{1,0:T(8,128)(2,1)}) %reduce-scatter.7.cloned.1.call-update) | async-done | bytes 393232 | tf_op jit(solution)/shard_map/reduce_scatter | solution.py:67
  621.5 0.0 copy-done.3
  621.5 1.8 add_convert_fusion.1
  623.4 2.3 fusion.21
  (26 shorter events, 0.1 us)
Async XLA Ops:
  7.2 129.4 %all-gather.6.cloned.1.call-start = ((), (), s32[]{:S(2)}) async-start(), calls=%async_computation.4 | async-start | bytes 3538944 | tf_op jit(solution)/shard_map/all_gather | solution.py:38
  7.9 236.5 %all-gather.10.cloned.1.call-start = ((), (), s32[]{:S(2)}) async-start(), calls=%async_computation.8 | async-start | bytes 3538944 | tf_op jit(solution)/shard_map/all_gather | solution.py:39
  8.6 268.0 %reduce-scatter.5.cloned.1.call-start = ((), (), s32[]{:S(2)}) async-start(), calls=%async_computation.5 | async-start | bytes 13762560 | tf_op jit(solution)/shard_map/reduce_scatter | solution.py:48
  19.4 36.2 %copy-start.7 = (s32[32,56]{1,0:T(8,128)S(1)}, s32[32,56]{1,0:T(8,128)}, u32[]{:S(2)}) copy-start(s32[32,56]{1,0:T(8,128)} %param.14) | copy-start | bytes 21508
  102.1 19.7 %copy-start = (bf16[2048,3584]{1,0:T(8,128)(2,1)S(1)}, bf16[2048,3584]{1,0:T(8,128)(2,1)}, u32[]{:S(2)}) copy-start(bf16[2048,3584]{1,0:T(8,128)(2,1)} %mul.140) | copy-start | bytes 44040196
  121.8 26.2 %copy-start.5 = (f32[2048]{0:T(1024)S(1)}, f32[2048]{0:T(1024)}, u32[]{:S(2)}) copy-start(f32[2048]{0:T(1024)} %param.10) | copy-start | bytes 24580
  136.6 29.0 %slice-start = ((s8[14680064]{0:T(1024)(128)(4,1)}), s8[2097152]{0:T(1024)(128)(4,1)S(1)}, s32[]{:S(2)}) async-start(s8[14680064]{0:T(1024)(128)(4,1)} %bitcast.25), calls=%async_computation.13 | async-start | bytes 4194304
  148.1 17.5 %slice-start.1 = ((s8[14680064]{0:T(1024)(128)(4,1)}), s8[4194304]{0:T(1024)(128)(4,1)S(1)}, s32[]{:S(2)}) async-start(s8[14680064]{0:T(1024)(128)(4,1)} %bitcast.25), calls=%async_computation.14 | async-start | bytes 8388608
  148.1 17.5 %slice-start.2 = ((s8[14680064]{0:T(1024)(128)(4,1)}), s8[4194304]{0:T(1024)(128)(4,1)S(1)}, s32[]{:S(2)}) async-start(s8[14680064]{0:T(1024)(128)(4,1)} %bitcast.25), calls=%async_computation.15 | async-start | bytes 8388608
  148.1 17.5 %slice-start.3 = ((s8[14680064]{0:T(1024)(128)(4,1)}), s8[4194304]{0:T(1024)(128)(4,1)S(1)}, s32[]{:S(2)}) async-start(s8[14680064]{0:T(1024)(128)(4,1)} %bitcast.25), calls=%async_computation.16 | async-start | bytes 8388608
  148.1 17.5 %copy-start.1 = (bf16[768,2048]{1,0:T(8,128)(2,1)S(1)}, bf16[768,2048]{1,0:T(8,128)(2,1)}, u32[]{:S(2)}) copy-start(bf16[768,2048]{1,0:T(8,128)(2,1)} %all-gather.6.cloned.1.call-done) | copy-start | bytes 9437188
  188.6 0.7 copy-start.8
  188.6 143.5 %reduce-scatter.9.cloned.1.call-start = ((), (), s32[]{:S(2)}) async-start(), calls=%async_computation.9 | async-start | bytes 6881280 | tf_op jit(solution)/shard_map/reduce_scatter | solution.py:76
  264.2 115.1 %all-gather.12.cloned.1.call-start = ((), (), s32[]{:S(2)}) async-start(), calls=%async_computation.10 | async-start | bytes 6881280 | tf_op jit(solution)/shard_map/all_gather | solution.py:87
  337.1 85.4 %all-gather.14.cloned.1.call-start = ((), (), s32[]{:S(2)}) async-start(), calls=%async_computation.11 | async-start | bytes 6881280 | tf_op jit(solution)/shard_map/all_gather | solution.py:88
  337.7 128.3 %all-gather.8.cloned.1.call-start = ((), (), s32[]{:S(2)}) async-start(), calls=%async_computation.6 | async-start | bytes 6881280 | tf_op jit(solution)/shard_map/all_gather | solution.py:65
  338.5 205.5 %reduce-scatter.11.cloned.1.call-start = ((), (), s32[]{:S(2)}) async-start(), calls=%async_computation.12 | async-start | bytes 3538944 | tf_op jit(solution)/shard_map/reduce_scatter | solution.py:92
  397.5 44.6 %copy-start.2 = (bf16[768,2048]{1,0:T(8,128)(2,1)S(1)}, bf16[768,2048]{1,0:T(8,128)(2,1)}, u32[]{:S(2)}) copy-start(bf16[768,2048]{1,0:T(8,128)(2,1)} %all-gather.6.cloned.1.call-done) | copy-start | bytes 9437188
  441.1 180.4 %reduce-scatter.7.cloned.1.call-start = ((), (), s32[]{:S(2)}) async-start(), calls=%async_computation.7 | async-start | bytes 3538944 | tf_op jit(solution)/shard_map/reduce_scatter | solution.py:67
  445.2 40.5 %copy-start.6 = (f32[2048]{0:T(1024)S(1)}, f32[2048]{0:T(1024)}, u32[]{:S(2)}) copy-start(f32[2048]{0:T(1024)} %param.10) | copy-start | bytes 24580
  523.1 98.4 %copy-start.3 = (bf16[96,2048]{1,0:T(8,128)(2,1)S(1)}, bf16[96,2048]{1,0:T(8,128)(2,1)}, u32[]{:S(2)}) copy-start(bf16[96,2048]{1,0:T(8,128)(2,1)} %param.9) | copy-start | bytes 1179652
  523.1 100.2 %copy-start.4 = (bf16[96,2048]{1,0:T(8,128)(2,1)S(1)}, bf16[96,2048]{1,0:T(8,128)(2,1)}, u32[]{:S(2)}) copy-start(bf16[96,2048]{1,0:T(8,128)(2,1)} %param.17) | copy-start | bytes 1179652
Sparse Core Ops, SparseCore 0:
  10.2 62.7 all-gather.5
  75.1 58.7 all-gather.9
  188.7 87.8 reduce-scatter.4
  279.1 53.0 reduce-scatter.8
  337.3 41.8 all-gather.11
  380.6 41.8 all-gather.13
  424.1 41.8 all-gather.7
  469.6 74.3 reduce-scatter.10
  547.6 73.8 reduce-scatter.6
where the time goes:
time: 644 us; the launch traced here: 632 us
  waiting for transfers between devices  201 us (31%)
  matrix products  165 us (26%)
  local copies, waits for them, and re-layouts  150 us (23%)
  other arithmetic  65.4 us (10%)
  blocking collectives  36.3 us (6%)
  between operations  14.2 us (2%)
    mul x6, local copies, waits for them, and re-layouts, expand_mask(): weight.reshape(mask_rows, BLOCK, mask_cols, BLOCK)  148 us
    dot_general x3, matrix products, contract_rows(): lax.dot_general(left, right, (((0,), (0,)), ((), ())), preferred_element_...  57.6 us
    dot_general x3, matrix products, contract_cols(): lax.dot_general(left, right, (((1,), (1,)), ((), ())), preferred_element_...  56.6 us
    reduce_scatter x1, waiting for transfers between devices, shards(): lax.psum_scatter(contract_cols(row_block, down_eff).astype(jnp.bfloat16),...  50.6 us
    reduce_scatter x1, waiting for transfers between devices, shards(): lax.psum_scatter(jnp.dot(row_block, down_eff, preferred_element_type=jnp....  47.9 us
    all_gather x1, waiting for transfers between devices, shards(): lax.all_gather(d_gate, 'col', axis=0, tiled=True)  40.7 us
    mul x2, other arithmetic, expand_mask(): weight.reshape(mask_rows, BLOCK, mask_cols, BLOCK)  33.3 us
    all_gather x1, waiting for transfers between devices, shards(): lax.all_gather(d_up, 'col', axis=0, tiled=True)  25.1 us
  transfers between devices with their start and end apart: 9, of which 7 were waited for; matrix products, arithmetic and copies ran while one was open for 58% of the time, Pallas kernels for 0%

commit v1 on v0

--- a/solution.py
+++ b/solution.py
@@ -6,6 +6,19 @@
 D = 8192
 BLOCK = 64
 epsilon = 1e-05
+
+
+def gather_around(x, axis, dim):
+    count, mine, rows = (lax.axis_size(axis), lax.axis_index(axis), x.shape[dim])
+    upward = [(i, (i + 1) % count) for i in range(count)]
+    filled = jnp.zeros((*x.shape[:dim], count * rows, *x.shape[dim + 1 :]), x.dtype)
+    carried = x
+    for lap in range(count):
+        source = (mine - lap) % count
+        filled = lax.dynamic_update_slice_in_dim(filled, carried, source * rows, axis=dim)
+        if lap < count - 1:
+            carried = lax.ppermute(carried, axis, upward)
+    return filled
 
 
 def expand_mask(weight, block_mask):
@@ -84,7 +97,7 @@
         d_hidden * up_value * sigmoid_gate * (1.0 + gate_value * (1.0 - sigmoid_gate))
     ).astype(jnp.bfloat16)
     d_gate_all, d_up_all = (
-        lax.all_gather(d_gate, "col", axis=0, tiled=True),
+        gather_around(d_gate, "col", 0),
         lax.all_gather(d_up, "col", axis=0, tiled=True),
     )
     grad_w_gate = expand_mask(contract_rows(hidden_in, d_gate_all).astype(jnp.bfloat16), mask_gate)

time: 644 us -> 650 us (level)
  local copies, waits for them, and re-layouts: 150 us -> 160 us
  waiting for transfers between devices: 201 us -> 193 us
    ppermute x0 -> x3, waiting for transfers between devices: none -> 88.5 us  [gather_around(): carried = lax.ppermute(carried, axis, upward)]
    all_gather x1 -> x0, waiting for transfers between devices: 40.7 us -> none  [shards(): lax.all_gather(d_gate, 'col', axis=0, tiled=True)]
    all_gather x1, waiting for transfers between devices: 25.1 us -> 0.01 us  [shards(): lax.all_gather(d_up, 'col', axis=0, tiled=True)]
    all_gather x1, waiting for transfers between devices: 20.8 us -> 0.01 us  [shards(): hidden_all = lax.all_gather(hidden, 'col', axis=0, tiled=True)]
    reduce_scatter x1, waiting for transfers between devices: 47.9 us -> 40.1 us  [shards(): lax.psum_scatter(jnp.dot(row_block, down_eff, preferred_element_type=jnp....]
  transfers between devices with their start and end apart: 9 -> 11, of which waited for: 7 -> 6; matrix products, arithmetic and copies ran while one was open for 58% -> 59% of each run, Pallas kernels for 0% -> 0%
where the time goes in v1:
time: 650 us; the launch traced here: 639 us
  waiting for transfers between devices  193 us (30%)
  matrix products  165 us (25%)
  local copies, waits for them, and re-layouts  160 us (25%)
  other arithmetic  67.2 us (10%)
  blocking collectives  37 us (6%)
  between operations  14.8 us (2%)
    mul x6, local copies, waits for them, and re-layouts, expand_mask(): weight.reshape(mask_rows, BLOCK, mask_cols, BLOCK)  148 us
    ppermute x3, waiting for transfers between devices, gather_around(): carried = lax.ppermute(carried, axis, upward)  88.5 us
    dot_general x3, matrix products, contract_rows(): lax.dot_general(left, right, (((0,), (0,)), ((), ())), preferred_element_...  57.6 us
    dot_general x3, matrix products, contract_cols(): lax.dot_general(left, right, (((1,), (1,)), ((), ())), preferred_element_...  56.7 us
    reduce_scatter x1, waiting for transfers between devices, shards(): lax.psum_scatter(contract_cols(row_block, down_eff).astype(jnp.bfloat16),...  50.7 us
    reduce_scatter x1, waiting for transfers between devices, shards(): lax.psum_scatter(jnp.dot(row_block, down_eff, preferred_element_type=jnp....  40.1 us
    mul x2, other arithmetic, expand_mask(): weight.reshape(mask_rows, BLOCK, mask_cols, BLOCK)  33.3 us
    psum x1, blocking collectives, shards(): grad_gain = lax.psum(gain_part, 'row')  23.2 us
  transfers between devices with their start and end apart: 11, of which 6 were waited for; matrix products, arithmetic and copies ran while one was open for 59% of the time, Pallas kernels for 0%

profile of v1, /device:TPU:0, one launch (start us, length us, event | category | flops | bytes accessed | tf_op | source)
XLA Modules:
  0.0 638.6 jit_solution(18122712579947246461)
XLA Ops:
  7.2 0.0 all-gather.5.cloned.1.call-start
  7.2 0.7 all-gather.5.cloned.1.call-update
  7.9 0.0 all-gather.9.cloned.1.call-start
  7.9 0.7 all-gather.9.cloned.1.call-update
  8.6 0.0 reduce-scatter.5.cloned.1.call-start
  8.7 0.7 convert_element_type.77
  9.4 10.0 %mul.154 = bf16[32,64,56,64]{3,2,1,0:T(8,128)(2,1)} broadcast(bf16[32,56]{1,0:T(8,128)(2,1)S(1)} %convert_element_type.77), dimensions={0,2} | broadcast | bytes 14683648 | tf_op jit(solution)/shard_map/mul | solution.py:27
  19.4 36.2 %mul.155 = bf16[2048,3584]{1,0:T(8,128)(2,1)} reshape(bf16[32,64,56,64]{3,2,1,0:T(8,128)(2,1)} %mul.154) | data formatting | bytes 29360128 | tf_op jit(solution)/shard_map/mul | solution.py:27
  55.7 10.2 %mul.151 = bf16[32,64,56,64]{3,2,1,0:T(8,128)(2,1)} broadcast(bf16[32,56]{1,0:T(8,128)(2,1)S(1)} %convert_element_type.76), dimensions={0,2} | broadcast | bytes 14683648 | tf_op jit(solution)/shard_map/mul | solution.py:27
  65.8 36.2 %mul.152 = bf16[2048,3584]{1,0:T(8,128)(2,1)} reshape(bf16[32,64,56,64]{3,2,1,0:T(8,128)(2,1)} %mul.151) | data formatting | bytes 29360128 | tf_op jit(solution)/shard_map/mul | solution.py:27
  102.1 18.6 %mul.156 = bf16[2048,3584]{1,0:T(8,128)(2,1)} multiply(bf16[2048,3584]{1,0:T(8,128)(2,1)} %param.12, bf16[2048,3584]{1,0:T(8,128)(2,1)} %mul.155) | non-fusion elementwise | flops 7340032 | bytes 44040192 | tf_op jit(solution)/shard_map/mul | solution.py:27
  120.7 1.1 copy-done
  121.8 14.7 %mul.153 = bf16[2048,3584]{1,0:T(8,128)(2,1)} multiply(bf16[2048,3584]{1,0:T(8,128)(2,1)} %param.11, bf16[2048,3584]{1,0:T(8,128)(2,1)S(1)} %copy-done) | non-fusion elementwise | flops 7340032 | bytes 44040192 | tf_op jit(solution)/shard_map/mul | solution.py:27
  136.5 2.7 fusion.3
  139.3 8.1 %psum.21 = f32[768,1]{0,1:T(1,128)S(1)} all-reduce(f32[768,1]{0,1:T(1,128)S(1)} %broadcast_in_dim.6), channel_id=1, replica_groups=mesh['row'=8,'col'=4] {'col'}, use_global_device_ids=true, to_apply=%region_1.0 | all-reduce | flops 768 | bytes 6144 | tf_op jit(solution)/shard_map/psum | solution.py:56
  147.3 0.6 fusion.25
  147.9 17.5 %convolution_convert_fusion.4 = bf16[768,3584]{1,0:T(8,128)(2,1)} fusion(bf16[2048,3584]{1,0:T(8,128)(2,1)} %mul.156, f32[2048]{0:T(1024)S(1)} %copy-done.8, f32[768]{0:T(1024)S(1)} %get-tuple-element.10, bf16[768,2048]{1,0:T(8,128)(2,1)} %all-gather.5.cloned.1.call-done), kind=kOutput, calls=%fused_computation.10 | convolution fusion | flops 11283333120 | bytes 23342080 | tf_op jit(solution)/shard_map/dot_general | solution.py:65
  165.5 13.5 %convolution_convert_fusion.5 = bf16[768,3584]{1,0:T(8,128)(2,1)} fusion(bf16[2048,3584]{1,0:T(8,128)(2,1)S(1)} %bitcast.26, f32[2048]{0:T(1024)S(1)} %copy-done.8, f32[768]{0:T(1024)S(1)} %get-tuple-element.10, bf16[768,2048]{1,0:T(8,128)(2,1)S(1)} %copy-done.2), kind=kOutput, calls=%fused_computation.11 | convolution fusion | flops 11283333120 | bytes 23342080 | tf_op jit(solution)/shard_map/dot_general | solution.py:64
  179.0 9.5 %pad_maximum_fusion = bf16[768,7168]{1,0:T(8,128)(2,1)} fusion(bf16[768,3584]{1,0:T(8,128)(2,1)} %convolution_convert_fusion.4, bf16[768,3584]{1,0:T(8,128)(2,1)} %convolution_convert_fusion.5), kind=kLoop, calls=%fused_computation.6 | loop fusion | flops 22020096 | bytes 22020096 | tf_op jit(solution)/shard_map/concatenate | solution.py:62
  188.5 0.0 reduce-scatter.5.cloned.1.call-update
  188.5 0.2 reduce-scatter.9.cloned.1.call-start
  188.7 0.5 copy-done.11
  189.2 0.1 copy.15
  189.3 14.1 %mul.159 = bf16[56,64,32,64]{3,2,1,0:T(8,128)(2,1)} broadcast(bf16[56,32]{1,0:T(8,128)(2,1)S(1)} %copy.15), dimensions={0,2} | broadcast | bytes 14683648 | tf_op jit(solution)/shard_map/mul | solution.py:27
  203.4 40.8 %mul.160 = bf16[3584,2048]{1,0:T(8,128)(2,1)} reshape(bf16[56,64,32,64]{3,2,1,0:T(8,128)(2,1)} %mul.159) | data formatting | bytes 29360128 | tf_op jit(solution)/shard_map/mul | solution.py:27
  244.2 19.8 %fusion.4 = bf16[768,3584]{1,0:T(8,128)(2,1)} fusion(bf16[768,2048]{1,0:T(8,128)(2,1)} %all-gather.9.cloned.1.call-done, bf16[3584,2048]{1,0:T(8,128)(2,1)} %param.13, bf16[3584,2048]{1,0:T(8,128)(2,1)} %mul.160), kind=kOutput, calls=%fused_computation.15 | convolution fusion | flops 11284381696 | bytes 38010880 | tf_op jit(solution)/shard_map/dot_general | solution.py:40
  264.1 0.0 reduce-scatter.9.cloned.1.call-update
  264.1 0.0 all-gather.11.cloned.1.call-start
  264.1 12.4 %reduce-scatter.5.cloned.1.call-done = bf16[192,7168]{1,0:T(8,128)(2,1)} async-done(((bf16[768,7168]{1,0:T(8,128)(2,1)}), bf16[192,7168]{1,0:T(8,128)(2,1)}) %reduce-scatter.5.cloned.1.call-update) | async-done | bytes 2752528 | tf_op jit(solution)/shard_map/reduce_scatter | solution.py:61
  276.6 4.8 convert_element_type.78
  281.4 50.7 %reduce-scatter.9.cloned.1.call-done = bf16[192,3584]{1,0:T(8,128)(2,1)} async-done(((bf16[768,3584]{1,0:T(8,128)(2,1)}), bf16[192,3584]{1,0:T(8,128)(2,1)}) %reduce-scatter.9.cloned.1.call-update) | async-done | bytes 1376272 | tf_op jit(solution)/shard_map/reduce_scatter | solution.py:89
  332.0 5.5 fusion.14
  337.6 0.0 all-gather.11.cloned.1.call-update
  337.6 0.0 all-gather.7.cloned.1.call-start
  337.7 0.4 broadcast_in_dim.7
  338.0 0.9 copy-done.4
  338.9 1.7 copy-done.1
  340.6 1.2 constant_dynamic-update-slice_fusion.3
  341.8 2.4 copy-done.5
  344.2 44.6 %collective-permute-done = bf16[192,3584]{1,0:T(8,128)(2,1)S(1)} collective-permute-done((bf16[192,3584]{1,0:T(8,128)(2,1)S(1)}, bf16[192,3584]{1,0:T(8,128)(2,1)S(1)}, u32[]{:S(2)}, u32[]{:S(2)}) %collective-permute-start) | collective-permute-done | bytes 1376288 | tf_op jit(solution)/shard_map/ppermute | solution.py:20
  388.8 17.7 %collective-permute-done.1 = bf16[192,3584]{1,0:T(8,128)(2,1)S(1)} collective-permute-done((bf16[192,3584]{1,0:T(8,128)(2,1)S(1)}, bf16[192,3584]{1,0:T(8,128)(2,1)S(1)}, u32[]{:S(2)}, u32[]{:S(2)}) %collective-permute-start.1) | collective-permute-done | bytes 1376288 | tf_op jit(solution)/shard_map/ppermute | solution.py:20
  406.5 0.0 all-gather.7.cloned.1.call-update
  406.5 0.3 reduce-scatter.11.cloned.1.call-start
  406.8 1.2 constant_dynamic-update-slice_fusion.2
  408.0 1.2 constant_dynamic-update-slice_fusion.1
  409.2 26.2 %collective-permute-done.2 = bf16[192,3584]{1,0:T(8,128)(2,1)} collective-permute-done((bf16[192,3584]{1,0:T(8,128)(2,1)S(1)}, bf16[192,3584]{1,0:T(8,128)(2,1)}, u32[]{:S(2)}, u32[]{:S(2)}) %collective-permute-start.2) | collective-permute-done | bytes 1376288 | tf_op jit(solution)/shard_map/ppermute | solution.py:20
  435.4 2.5 constant_dynamic-update-slice_fusion
  437.9 18.2 %fusion.26 = f32[768,2048]{1,0:T(8,128)} fusion(bf16[768,3584]{1,0:T(8,128)(2,1)} %all-gather.11.cloned.1.call-done, bf16[2048,3584]{1,0:T(8,128)(2,1)} %mul.156), kind=kOutput, calls=%fused_computation.48 | convolution fusion | flops 11274289152 | bytes 26476544 | tf_op jit(solution)/shard_map/dot_general | solution.py:40
  456.1 18.7 %add_convert_fusion = bf16[768,2048]{1,0:T(8,128)(2,1)} fusion(f32[768,2048]{1,0:T(8,128)} %fusion.26, bf16[768,3584]{1,0:T(8,128)(2,1)} %constant_dynamic-update-slice_fusion, bf16[2048,3584]{1,0:T(8,128)(2,1)} %mul.153), kind=kOutput, calls=%fused_computation.13 | convolution fusion | flops 11277434880 | bytes 29622272 | tf_op jit(solution)/shard_map/dot_general | solution.py:40
  474.7 0.0 reduce-scatter.11.cloned.1.call-update
  474.8 0.3 reduce-scatter.7.cloned.1.call-start
  475.1 0.8 fusion.23
  475.8 3.1 convert_multiply_fusion
  479.0 20.0 %fusion.8 = bf16[768,2048]{1,0:T(8,128)(2,1)} fusion(bf16[768,3584]{1,0:T(8,128)(2,1)} %all-gather.7.cloned.1.call-done, bf16[3584,2048]{1,0:T(8,128)(2,1)} %param.13, bf16[3584,2048]{1,0:T(8,128)(2,1)} %mul.160), kind=kOutput, calls=%fused_computation.21 | convolution fusion | flops 11283202048 | bytes 38010880 | tf_op jit(solution)/shard_map/dot_general | solution.py:81
  499.0 0.0 reduce-scatter.7.cloned.1.call-update
  499.0 18.8 %fusion = bf16[2048,3584]{1,0:T(8,128)(2,1)} fusion(bf16[2048,3584]{1,0:T(8,128)(2,1)} %mul.152, bf16[768,3584]{1,0:T(8,128)(2,1)} %constant_dynamic-update-slice_fusion, f32[2048]{0:T(1024)S(1)} %copy-done.9, f32[768]{0:T(1024)S(1)} %get-tuple-element.10, bf16[768,2048]{1,0:T(8,128)(2,1)S(1)} %copy-done.3), kind=kOutput, calls=%fused_computation.3 | convolution fusion | flops 11295260672 | bytes 38022144 | tf_op jit(solution)/shard_map/dot_general | solution.py:34
  517.8 18.7 %fusion.1 = bf16[2048,3584]{1,0:T(8,128)(2,1)} fusion(bf16[2048,3584]{1,0:T(8,128)(2,1)} %mul.155, bf16[768,3584]{1,0:T(8,128)(2,1)} %all-gather.11.cloned.1.call-done, f32[2048]{0:T(1024)S(1)} %copy-done.9, f32[768]{0:T(1024)S(1)} %get-tuple-element.10, bf16[768,2048]{1,0:T(8,128)(2,1)S(1)} %copy-done.3), kind=kOutput, calls=%fused_computation.4 | convolution fusion | flops 11295260672 | bytes 38022144 | tf_op jit(solution)/shard_map/dot_general | solution.py:34
  536.4 20.2 %fusion.2 = bf16[3584,2048]{1,0:T(8,128)(2,1)} fusion(bf16[3584,2048]{1,0:T(8,128)(2,1)} %mul.160, bf16[768,3584]{1,0:T(8,128)(2,1)} %all-gather.7.cloned.1.call-done, bf16[768,2048]{1,0:T(8,128)(2,1)} %all-gather.9.cloned.1.call-done), kind=kOutput, calls=%fused_computation.5 | convolution fusion | flops 11288969216 | bytes 38010880 | tf_op jit(solution)/shard_map/dot_general | solution.py:34
  556.6 1.5 fusion.22
  558.1 5.7 psum.22
  563.8 23.2 %psum.23 = f32[2048]{0:T(1024)} all-reduce(f32[2048]{0:T(1024)S(1)} %get-tuple-element.6), channel_id=1, replica_groups=mesh['row'=8,'col'=4] {'row'}, use_global_device_ids=true, to_apply=%region_9.10 | all-reduce | flops 2048 | bytes 16384 | tf_op jit(solution)/shard_map/psum | solution.py:120
  587.0 40.1 %reduce-scatter.7.cloned.1.call-done = bf16[96,2048]{1,0:T(8,128)(2,1)} async-done(((bf16[768,2048]{1,0:T(8,128)(2,1)}), bf16[96,2048]{1,0:T(8,128)(2,1)}) %reduce-scatter.7.cloned.1.call-update) | async-done | bytes 393232 | tf_op jit(solution)/shard_map/reduce_scatter | solution.py:80
  627.2 1.8 add_convert_fusion.1
  629.0 2.3 fusion.21
  (40 shorter events, 0.1 us)
Async XLA Ops:
  7.2 129.4 %all-gather.5.cloned.1.call-start = ((), (), s32[]{:S(2)}) async-start(), calls=%async_computation.4 | async-start | bytes 3538944 | tf_op jit(solution)/shard_map/all_gather | solution.py:51
  7.9 236.3 %all-gather.9.cloned.1.call-start = ((), (), s32[]{:S(2)}) async-start(), calls=%async_computation.8 | async-start | bytes 3538944 | tf_op jit(solution)/shard_map/all_gather | solution.py:52
  8.6 267.9 %reduce-scatter.5.cloned.1.call-start = ((), (), s32[]{:S(2)}) async-start(), calls=%async_computation.5 | async-start | bytes 13762560 | tf_op jit(solution)/shard_map/reduce_scatter | solution.py:61
  19.4 36.2 %copy-start.10 = (s32[32,56]{1,0:T(8,128)S(1)}, s32[32,56]{1,0:T(8,128)}, u32[]{:S(2)}) copy-start(s32[32,56]{1,0:T(8,128)} %param.14) | copy-start | bytes 21508
  102.1 19.7 %copy-start = (bf16[2048,3584]{1,0:T(8,128)(2,1)S(1)}, bf16[2048,3584]{1,0:T(8,128)(2,1)}, u32[]{:S(2)}) copy-start(bf16[2048,3584]{1,0:T(8,128)(2,1)} %mul.152) | copy-start | bytes 44040196
  121.8 26.1 %copy-start.8 = (f32[2048]{0:T(1024)S(1)}, f32[2048]{0:T(1024)}, u32[]{:S(2)}) copy-start(f32[2048]{0:T(1024)} %param.10) | copy-start | bytes 24580
  136.5 28.9 %slice-start = ((s8[14680064]{0:T(1024)(128)(4,1)}), s8[2097152]{0:T(1024)(128)(4,1)S(1)}, s32[]{:S(2)}) async-start(s8[14680064]{0:T(1024)(128)(4,1)} %bitcast.25), calls=%async_computation.12 | async-start | bytes 4194304
  147.9 17.5 %slice-start.1 = ((s8[14680064]{0:T(1024)(128)(4,1)}), s8[4194304]{0:T(1024)(128)(4,1)S(1)}, s32[]{:S(2)}) async-start(s8[14680064]{0:T(1024)(128)(4,1)} %bitcast.25), calls=%async_computation.13 | async-start | bytes 8388608
  147.9 17.5 %slice-start.2 = ((s8[14680064]{0:T(1024)(128)(4,1)}), s8[4194304]{0:T(1024)(128)(4,1)S(1)}, s32[]{:S(2)}) async-start(s8[14680064]{0:T(1024)(128)(4,1)} %bitcast.25), calls=%async_computation.14 | async-start | bytes 8388608
  147.9 17.5 %slice-start.3 = ((s8[14680064]{0:T(1024)(128)(4,1)}), s8[4194304]{0:T(1024)(128)(4,1)S(1)}, s32[]{:S(2)}) async-start(s8[14680064]{0:T(1024)(128)(4,1)} %bitcast.25), calls=%async_computation.15 | async-start | bytes 8388608
  147.9 17.5 %copy-start.2 = (bf16[768,2048]{1,0:T(8,128)(2,1)S(1)}, bf16[768,2048]{1,0:T(8,128)(2,1)}, u32[]{:S(2)}) copy-start(bf16[768,2048]{1,0:T(8,128)(2,1)} %all-gather.5.cloned.1.call-done) | copy-start | bytes 9437188
  188.5 0.7 copy-start.11
  188.5 143.5 %reduce-scatter.9.cloned.1.call-start = ((), (), s32[]{:S(2)}) async-start(), calls=%async_computation.9 | async-start | bytes 6881280 | tf_op jit(solution)/shard_map/reduce_scatter | solution.py:89
  264.1 173.8 %all-gather.11.cloned.1.call-start = ((), (), s32[]{:S(2)}) async-start(), calls=%async_computation.10 | async-start | bytes 6881280 | tf_op jit(solution)/shard_map/all_gather | solution.py:101
  337.5 1.3 copy-start.4
  337.6 141.4 %all-gather.7.cloned.1.call-start = ((), (), s32[]{:S(2)}) async-start(), calls=%async_computation.6 | async-start | bytes 6881280 | tf_op jit(solution)/shard_map/all_gather | solution.py:78
  337.6 2.9 copy-start.1
  341.8 2.4 copy-start.5
  344.2 44.6 %collective-permute-start = (bf16[192,3584]{1,0:T(8,128)(2,1)S(1)}, bf16[192,3584]{1,0:T(8,128)(2,1)S(1)}, u32[]{:S(2)}, u32[]{:S(2)}) collective-permute-start(bf16[192,3584]{1,0:T(8,128)(2,1)S(1)} %get-tuple-element.9), channel_id=1, source_target_pairs={{0,1},{1,2},{2,3},{3,0},{4,5},{5,6},{6,7},{7,4},{8,9},{9,10},{10,1... | collective-permute-start | bytes 4128776 | tf_op jit(solution)/shard_map/ppermute | solution.py:20
  388.8 17.7 %collective-permute-start.1 = (bf16[192,3584]{1,0:T(8,128)(2,1)S(1)}, bf16[192,3584]{1,0:T(8,128)(2,1)S(1)}, u32[]{:S(2)}, u32[]{:S(2)}) collective-permute-start(bf16[192,3584]{1,0:T(8,128)(2,1)S(1)} %collective-permute-done), channel_id=1, source_target_pairs={{0,1},{1,2},{2,3},{3,0},{4,5},{5,6},{6,7},{7,4},{8,9},{9,10},{10,1... | collective-permute-start | bytes 4128776 | tf_op jit(solution)/shard_map/ppermute | solution.py:20
  406.5 28.8 %collective-permute-start.2 = (bf16[192,3584]{1,0:T(8,128)(2,1)S(1)}, bf16[192,3584]{1,0:T(8,128)(2,1)}, u32[]{:S(2)}, u32[]{:S(2)}) collective-permute-start(bf16[192,3584]{1,0:T(8,128)(2,1)S(1)} %collective-permute-done.1), channel_id=1, source_target_pairs={{0,1},{1,2},{2,3},{3,0},{4,5},{5,6},{6,7},{7,4},{8,9},{9,10},{10,1... | collective-permute-start | bytes 4128776 | tf_op jit(solution)/shard_map/ppermute | solution.py:20
  406.5 150.1 %reduce-scatter.11.cloned.1.call-start = ((), (), s32[]{:S(2)}) async-start(), calls=%async_computation.11 | async-start | bytes 3538944 | tf_op jit(solution)/shard_map/reduce_scatter | solution.py:105
  456.1 19.8 %copy-start.3 = (bf16[768,2048]{1,0:T(8,128)(2,1)S(1)}, bf16[768,2048]{1,0:T(8,128)(2,1)}, u32[]{:S(2)}) copy-start(bf16[768,2048]{1,0:T(8,128)(2,1)} %all-gather.5.cloned.1.call-done) | copy-start | bytes 9437188
  474.8 152.4 %reduce-scatter.7.cloned.1.call-start = ((), (), s32[]{:S(2)}) async-start(), calls=%async_computation.7 | async-start | bytes 3538944 | tf_op jit(solution)/shard_map/reduce_scatter | solution.py:80
  479.0 20.0 %copy-start.9 = (f32[2048]{0:T(1024)S(1)}, f32[2048]{0:T(1024)}, u32[]{:S(2)}) copy-start(f32[2048]{0:T(1024)} %param.10) | copy-start | bytes 24580
  536.4 90.7 %copy-start.6 = (bf16[96,2048]{1,0:T(8,128)(2,1)S(1)}, bf16[96,2048]{1,0:T(8,128)(2,1)}, u32[]{:S(2)}) copy-start(bf16[96,2048]{1,0:T(8,128)(2,1)} %param.9) | copy-start | bytes 1179652
  536.4 92.6 %copy-start.7 = (bf16[96,2048]{1,0:T(8,128)(2,1)S(1)}, bf16[96,2048]{1,0:T(8,128)(2,1)}, u32[]{:S(2)}) copy-start(bf16[96,2048]{1,0:T(8,128)(2,1)} %param.17) | copy-start | bytes 1179652
Sparse Core Ops, SparseCore 0:
  10.2 62.7 all-gather.4
  75.1 58.6 all-gather.8
  188.6 87.9 reduce-scatter.4
  279.0 53.0 reduce-scatter.8
  337.7 55.3 all-gather.10
  406.7 48.6 all-gather.6
  474.9 74.4 reduce-scatter.10
  553.0 74.1 reduce-scatter.6
